TPU v7x, 256 devices: a whole 4x4x8 slice. The times are simulated.
256 devices in a mesh: ctx: 64 (over z, y, core), tp: 4 (over x).
Axes of the slice: x: 4, y: 4, z: 8, core: 2. Of those that a mesh axis runs over, the one named last changes fastest.
Arguments:
- projected: bfloat16 [8192, 4, 4640], P('ctx', 'tp'), may hold values from -6 to 6
- conv_weight: float32 [4, 4, 2560], P('tp'), may hold values from -3 to 3
- conv_bias: float32 [4, 2560], P('tp'), may hold values from -1.5 to 1.5
- step_bias: float32 [4, 32], P('tp'), may hold values from -1 to 0.5
- log_rates: float32 [4, 32], P('tp'), as said below
- norm_gain: float32 [4, 2048], P('tp'), may hold values from 0.1 to 1.9
- out_weight: bfloat16 [4, 2048, 4096], P('tp', 'ctx'), may hold values from -0.0625 to 0.0625
Outputs:
- mixed: bfloat16 [8192, 4096], P('ctx', 'tp')
Inputs may be any that keep to these rules, and one draw needn't show every extreme that they name: log_rates lies between log(0.3 / 8192) and log(1 / 25).
All inputs are finite; a program needn't handle non-finite values.
Results may differ from a plain program's by a relative error of at most 0.0058.
Values may be sent and summed in bfloat16 or wider, within the bound.
No kernel may reach another device: no remote copies, remote signals or barrier semaphores. Data moves between devices by JAX's collectives and lax.ppermute only.
A program may use at most 320 MiB of HBM per device.

v0:
```python
import jax
import jax.numpy as jnp
import numpy as np
from jax import lax
from jax.sharding import PartitionSpec as P

P_SIZE = 64
N = 256
KCONV = 4
SPAN = 128
GCH = 2048
GCONV = 2560
highest_precision = lax.Precision.HIGHEST


def from_behind(shard, axis, by):
    peers = lax.axis_size(axis)
    pairs = [(i, i + by) for i in range(peers) if 0 <= i + by < peers]
    return lax.ppermute(shard, axis, pairs)


def ssd_blocks(inputs_x, step_sizes, decay_rate, b_keys, c_keys, block_rows):
    row_count = inputs_x.shape[0]
    block_count = row_count // block_rows
    head_count = inputs_x.shape[1]
    head_width = inputs_x.shape[2]
    state_count = b_keys.shape[1]
    x_blocks = inputs_x.reshape(block_count, block_rows, head_count, head_width)
    step_blocks = step_sizes.reshape(block_count, block_rows, head_count)
    b_blocks = b_keys.reshape(block_count, block_rows, state_count)
    c_blocks = c_keys.reshape(block_count, block_rows, state_count)
    causal_mask = (jnp.arange(block_rows)[:, None] >= jnp.arange(block_rows)[None, :])[None]

    def advance(carried, pieces):
        x_block, step_block, b_block, c_block = pieces
        log_steps = step_block * decay_rate[None, :]
        running = jnp.cumsum(log_steps, axis=0)
        intersection = jnp.dot(c_block, b_block.T, preferred_element_type=jnp.float32)
        b_float = b_block.astype(jnp.float32)
        c_float = c_block.astype(jnp.float32)
        log_gaps = running.T[:, :, None] - running.T[:, None, :]
        factors = jnp.where(causal_mask, jnp.exp(jnp.where(causal_mask, log_gaps, 0.0)), 0.0)
        factors = factors * intersection[None] * step_block.T[:, None, :]
        within = jnp.einsum("hts,shp->thp", factors, x_block, precision=highest_precision)
        carried_part = (
            jnp.einsum("tn,hpn->thp", c_float, carried, precision=highest_precision)
            * jnp.exp(running)[:, :, None]
        )
        tail_weight = jnp.exp(running[-1][None, :] - running) * step_block
        weighted = x_block * tail_weight[:, :, None]
        updated = carried * jnp.exp(running[-1])[:, None, None] + jnp.einsum(
            "shp,sn->hpn", weighted, b_float, precision=highest_precision
        )
        return (updated, within + carried_part)

    initial = jnp.zeros((head_count, head_width, state_count), jnp.float32)
    final_state, outputs = lax.scan(advance, initial, (x_blocks, step_blocks, b_blocks, c_blocks))
    total_log = jnp.sum(step_sizes * decay_rate[None, :], axis=0)
    return (outputs.reshape(row_count, head_count, head_width), final_state, total_log)


def on_device(projected, conv_weight, conv_bias, step_bias, log_rates, norm_gain, out_weight):
    row_count = projected.shape[0]
    conv_input = projected[:, :, GCH : GCH + GCONV]
    rim_rows = from_behind(conv_input[row_count - (KCONV - 1) :], "ctx", 1)
    padded = jnp.concatenate([rim_rows, conv_input], axis=0).astype(jnp.float32)
    mixed_conv = conv_bias[None]
    for offset in range(KCONV):
        mixed_conv = mixed_conv + conv_weight[:, offset][None] * padded[offset : offset + row_count]
    activated = jax.nn.silu(mixed_conv).astype(jnp.bfloat16)
    values = activated[:, :, :GCH]
    key_rows = activated[:, :, GCH:]
    raw_steps = projected[:, :, GCH + GCONV :]
    decay_rate = -jnp.exp(log_rates)
    devices = lax.axis_size("ctx")
    shard_width = GCH // devices
    shard_heads = max(1, shard_width // P_SIZE)
    piece_width = shard_width // shard_heads
    head_table = (
        np.arange(devices)[:, None] * shard_width // P_SIZE + np.arange(shard_heads)[None, :]
    ).reshape(-1)
    spread_steps = jnp.take(raw_steps, jnp.asarray(head_table, jnp.int32), axis=2)
    local_values, local_steps = (
        lax.all_to_all(values, "ctx", split_axis=2, concat_axis=0, tiled=True),
        lax.all_to_all(spread_steps, "ctx", split_axis=2, concat_axis=0, tiled=True),
    )
    all_keys = lax.all_gather(key_rows, "ctx", axis=0, tiled=True)
    sequence = local_values.shape[0]
    first_head = lax.axis_index("ctx") * shard_width // P_SIZE
    bias_slice = lax.dynamic_slice_in_dim(step_bias[0], first_head, shard_heads)
    rate_slice = lax.dynamic_slice_in_dim(decay_rate[0], first_head, shard_heads)
    step_sizes = jax.nn.softplus(local_steps[:, 0].astype(jnp.float32) + bias_slice[None, :])
    outputs, final_state, total_log = ssd_blocks(
        local_values[:, 0].astype(jnp.float32).reshape(sequence, shard_heads, piece_width),
        step_sizes,
        rate_slice,
        all_keys[:, 0, :N],
        all_keys[:, 0, N:],
        4 * SPAN,
    )
    pieces_out = [outputs.reshape(sequence, shard_width).astype(jnp.bfloat16)]
    scanned = lax.all_to_all(
        jnp.stack(pieces_out, axis=1), "ctx", split_axis=0, concat_axis=2, tiled=True
    )
    gated = scanned.astype(jnp.float32) * jax.nn.silu(projected[:, :, :GCH].astype(jnp.float32))
    normed = (
        gated * lax.rsqrt(jnp.mean(gated * gated, axis=2, keepdims=True) + 1e-05) * norm_gain[None]
    ).astype(jnp.bfloat16)
    summed = jnp.einsum(
        "tgr,grd->td",
        normed,
        lax.all_gather(out_weight, "ctx", axis=1, tiled=True),
        preferred_element_type=jnp.float32,
    )
    shares = lax.psum_scatter(summed, "tp", scatter_dimension=1, tiled=True)
    return shares.astype(jnp.bfloat16)


def solution(mesh):
    return jax.shard_map(
        on_device,
        mesh=mesh,
        in_specs=(
            P("ctx", "tp", None),
            P("tp", None, None),
            P("tp", None),
            P("tp", None),
            P("tp", None),
            P("tp", None),
            P("tp", "ctx", None),
        ),
        out_specs=P("ctx", "tp"),
        check_vma=False,
    )
```

profile of v0, /device:TPU:1, one launch (start us, length us, event | category | flops | bytes accessed | tf_op | source)
XLA Modules:
  0.0 387.9 jit_solution(16653090227472884516)
XLA Ops:
  6.5 1.4 slice.62
  8.2 4.7 %collective-permute-start = (bf16[3,1,2560]{2,0,1:T(4,128)(2,1)S(1)}, bf16[3,1,2560]{2,0,1:T(4,128)(2,1)S(1)}, u32[]{:S(2)}, u32[]{:S(2)}) collective-permute-start(bf16[3,1,2560]{2,0,1:T(4,128)(2,1)S(1)} %copy.77), channel_id=1, source_target_pairs={{0,4},{4,8},{8,12},{12,16},{16,20},{20,24},{24,28},{28,32},{32,36}... | collective-permute-start | bytes 46088 | tf_op jit(solution)/shard_map/ppermute | solution.py:19
  16.9 13.5 %all-to-all-start = ((bf16[128,1,64]{0,1,2:T(2,128)(2,1)}), bf16[128,1,64]{0,1,2:T(2,128)(2,1)S(1)}, u32[]{:S(2)}, u32[]{:S(2)}) async-start(bf16[128,1,64]{0,1,2:T(2,128)(2,1)} %copy.66), calls=%async_computation | async-start | bytes 65536 | tf_op jit(solution)/shard_map/all_to_all | solution.py:85
  31.7 11.5 %reduce.12 = bf16[2048,128]{1,0:T(8,128)(2,1)S(1)} reduce(bf16[2048,1,128]{2,1,0:T(2,128)(2,1)S(1)} %bitcast.163, bf16[]{:T(256)} %broadcast.159), dimensions={1}, to_apply=%bitcast.98.reduce_sub_computation | reduce | bytes 1048578
  44.2 10.3 %all-to-all-start.1 = ((bf16[64,2,2048]{2,1,0:T(2,128)(2,1)}), bf16[64,2,2048]{2,1,0:T(2,128)(2,1)S(1)}, u32[]{:S(2)}, u32[]{:S(2)}) async-start(bf16[64,2,2048]{2,1,0:T(2,128)(2,1)} %reshape.445), calls=%async_computation.1 | async-start | bytes 1048576 | tf_op jit(solution)/shard_map/all_to_all | solution.py:84
  57.5 14.9 %all-to-all-done.1 = bf16[64,2,2048]{2,1,0:T(2,128)(2,1)S(1)} async-done(((bf16[64,2,2048]{2,1,0:T(2,128)(2,1)}), bf16[64,2,2048]{2,1,0:T(2,128)(2,1)S(1)}, u32[]{:S(2)}, u32[]{:S(2)}) %all-to-all-start.1) | async-done | bytes 524320 | tf_op jit(solution)/shard_map/all_to_all | solution.py:84
  74.1 2.7 copy.70
  76.8 26.9 %all-gather.3.cloned.1.call-done = bf16[8192,1,512]{2,0,1:T(8,128)(2,1)} async-done(((bf16[128,1,512]{2,0,1:T(8,128)(2,1)}), bf16[8192,1,512]{2,0,1:T(8,128)(2,1)}) %all-gather.3.cloned.1.call-update) | async-done | bytes 8388624 | tf_op jit(solution)/shard_map/all_gather | solution.py:87
  103.7 5.9 %fusion.41 = (bf16[8192,1,256]{2,0,1:T(8,128)(2,1)}, bf16[8192,1,256]{2,0,1:T(8,128)(2,1)}) fusion(bf16[8192,1,512]{2,0,1:T(8,128)(2,1)} %all-gather.3.cloned.1.call-done), kind=kLoop, calls=%fused_computation.76 | loop fusion | bytes 16777216 | tf_op jit(solution)/shard_map/slice | solution.py:98
  109.6 184.8 %while.14 = (s32[]{:T(128)}, f32[1,32,256]{2,1,0:T(8,128)S(1)}, bf16[16,512,1,32]{1,3,2,0:T(8,128)(2,1)S(1)}, f32[16,512,1]{1,0,2:T(8,128)S(1)}, f32[1]{0:T(128)...) while((s32[]{:T(128)}, f32[1,32,256]{2,1,0:T(8,128)S(1)}, ...), condition=%wide.region_3.4_spmd.clone.clone, body=%wide.region_0.0_spmd.clone.clone.sunk | while | flops 337266176 | bytes 4002620 | solution.py:57
  113.5 2.4 broadcast_multiply_fusion.2
  115.9 1.4 fusion.69
  125.0 2.4 broadcast_multiply_fusion.2
  127.4 1.4 fusion.69
  136.5 2.4 broadcast_multiply_fusion.2
  139.0 1.4 fusion.69
  148.1 2.4 broadcast_multiply_fusion.2
  150.5 1.4 fusion.69
  154.3 1.4 fusion.67
  159.7 2.5 broadcast_multiply_fusion.2
  162.1 1.4 fusion.69
  166.0 1.4 fusion.67
  171.3 2.4 broadcast_multiply_fusion.2
  182.8 2.4 broadcast_multiply_fusion.2
  185.3 1.4 fusion.69
  194.4 2.4 broadcast_multiply_fusion.2
  206.0 2.4 broadcast_multiply_fusion.2
  217.5 2.4 broadcast_multiply_fusion.2
  229.1 2.4 broadcast_multiply_fusion.2
  240.6 2.4 broadcast_multiply_fusion.2
  243.0 1.4 fusion.69
  252.1 2.4 broadcast_multiply_fusion.2
  254.6 1.4 fusion.69
  263.7 2.4 broadcast_multiply_fusion.2
  266.1 1.4 fusion.69
  275.2 2.4 broadcast_multiply_fusion.2
  277.6 1.4 fusion.69
  286.7 2.4 broadcast_multiply_fusion.2
  289.1 1.4 fusion.69
  294.4 1.7 reduce.13
  296.0 1.9 copy.81
  298.0 2.8 reshape.447
  300.8 23.8 %all_to_all.12 = bf16[64,2,2048]{2,1,0:T(2,128)(2,1)S(1)} all-to-all(bf16[64,2,2048]{2,1,0:T(2,128)(2,1)} %reshape.447), channel_id=1, replica_groups=mesh['ctx'=64,'tp'=4] {'ctx'}, dimensions={0} | all-to-all | bytes 1048576 | tf_op jit(solution)/shard_map/all_to_all | solution.py:102
  324.6 7.1 %reshape.448 = bf16[8192,1,32]{2,1,0:T(2,128)(2,1)} reshape(bf16[64,2,2048]{2,1,0:T(2,128)(2,1)S(1)} %all_to_all.12) | data formatting | bytes 1048576
  331.8 8.0 %copy.74 = bf16[8192,1,32]{0,2,1:T(8,128)(2,1)S(1)} copy(bf16[8192,1,32]{2,1,0:T(2,128)(2,1)} %reshape.448) | data formatting | bytes 1048576 | tf_op jit(solution)/shard_map/all_to_all | solution.py:102
  341.3 9.6 %fusion.25 = f32[128,4096]{1,0:T(8,128)} fusion(bf16[1,2048,4096]{2,1,0:T(8,128)(2,1)} %all-gather.5.cloned.1.call-done, f32[128,1,2048]{0,2,1:T(8,128)S(1)} %get-tuple-element.150, f32[2048]{0:T(1024)S(1)} %bitcast.173, f32[128]{0:T(128)S(1)} %add_rsqrt_fusion), kind=kOutput, calls=%fused_computation.38 | convolution fusion | flops 2148270080 | bytes 19931648 | tf_op jit(solution)/shard_map/tgr,grd->td/dot_general | solution.py:109
  350.9 28.7 %reduce-scatter.2.cloned.1.call-done = f32[128,1024]{1,0:T(8,128)} async-done(((f32[128,4096]{1,0:T(8,128)}), f32[128,1024]{1,0:T(8,128)}) %reduce-scatter.2.cloned.1.call-update) | async-done | bytes 524304 | tf_op jit(solution)/shard_map/reduce_scatter | solution.py:115
  379.6 1.8 convert_element_type.107
  (271 shorter events, 118.4 us)
Async XLA Ops:
  6.5 49.0 %copy-start = (f32[1,32]{1,0:T(1,128)S(1)}, f32[1,32]{1,0:T(1,128)}, u32[]{:S(2)}) copy-start(f32[1,32]{1,0:T(1,128)} %param.13) | copy-start | bytes 388
  6.5 6.4 %copy-start.5 = (f32[1,4,2560]{2,1,0:T(4,128)S(1)}, f32[1,4,2560]{2,1,0:T(4,128)}, u32[]{:S(2)}) copy-start(f32[1,4,2560]{2,1,0:T(4,128)} %param.11) | copy-start | bytes 122884
  6.5 6.5 %slice-start = ((bf16[128,1,4640]{0,2,1:T(8,128)(2,1)}), bf16[128,1,2560]{0,2,1:T(8,128)(2,1)S(1)}, s32[]{:S(2)}) async-start(bf16[128,1,4640]{0,2,1:T(8,128)(2,1)} %param.10), calls=%async_computation.7 | async-start | bytes 1310720 | tf_op jit(solution)/shard_map/slice | solution.py:64
  6.5 97.2 %all-gather.3.cloned.1.call-start = ((), (), s32[]{:S(2)}) async-start(), calls=%async_computation.4 | async-start | bytes 8519680 | tf_op jit(solution)/shard_map/all_gather | solution.py:87
  8.2 5.1 %copy-start.6 = (f32[1,2560]{1,0:T(1,128)S(1)}, f32[1,2560]{1,0:T(1,128)}, u32[]{:S(2)}) copy-start(f32[1,2560]{1,0:T(1,128)} %param.12) | copy-start | bytes 30724
  8.2 5.6 %collective-permute-start = (bf16[3,1,2560]{2,0,1:T(4,128)(2,1)S(1)}, bf16[3,1,2560]{2,0,1:T(4,128)(2,1)S(1)}, u32[]{:S(2)}, u32[]{:S(2)}) collective-permute-start(bf16[3,1,2560]{2,0,1:T(4,128)(2,1)S(1)} %copy.77), channel_id=1, source_target_pairs={{0,4},{4,8},{8,12},{12,16},{16,20},{20,24},{24,28},{28,32},{32,36}... | collective-permute-start | bytes 46088 | tf_op jit(solution)/shard_map/ppermute | solution.py:19
  14.0 1.6 copy-start.7
  14.0 1.6 copy-start.2
  16.9 27.3 %all-to-all-start = ((bf16[128,1,64]{0,1,2:T(2,128)(2,1)}), bf16[128,1,64]{0,1,2:T(2,128)(2,1)S(1)}, u32[]{:S(2)}, u32[]{:S(2)}) async-start(bf16[128,1,64]{0,1,2:T(2,128)(2,1)} %copy.66), calls=%async_computation | async-start | bytes 65536 | tf_op jit(solution)/shard_map/all_to_all | solution.py:85
  43.2 13.0 %copy-start.8 = (f32[1,32]{1,0:T(1,128)S(1)}, f32[1,32]{1,0:T(1,128)}, u32[]{:S(2)}) copy-start(f32[1,32]{1,0:T(1,128)} %param.14) | copy-start | bytes 388
  44.2 28.2 %all-to-all-start.1 = ((bf16[64,2,2048]{2,1,0:T(2,128)(2,1)}), bf16[64,2,2048]{2,1,0:T(2,128)(2,1)S(1)}, u32[]{:S(2)}, u32[]{:S(2)}) async-start(bf16[64,2,2048]{2,1,0:T(2,128)(2,1)} %reshape.445), calls=%async_computation.1 | async-start | bytes 1048576 | tf_op jit(solution)/shard_map/all_to_all | solution.py:84
  54.5 286.5 %all-gather.5.cloned.1.call-start = ((), (), s32[]{:S(2)}) async-start(), calls=%async_computation.5 | async-start | bytes 17039360 | tf_op jit(solution)/shard_map/all_gather | solution.py:112
  55.3 324.3 %reduce-scatter.2.cloned.1.call-start = ((), (), s32[]{:S(2)}) async-start(), calls=%async_computation.6 | async-start | bytes 2621440 | tf_op jit(solution)/shard_map/reduce_scatter | solution.py:115
  76.8 32.8 %copy-start.3 = (bf16[16,512,1,32]{1,3,2,0:T(8,128)(2,1)S(1)}, bf16[16,512,1,32]{1,3,2,0:T(8,128)(2,1)}, u32[]{:S(2)}) copy-start(bf16[16,512,1,32]{1,3,2,0:T(8,128)(2,1)} %custom-call.3) | copy-start | bytes 1572868
  340.6 0.7 copy-start.4
  350.9 30.5 %copy-start.1 = (f32[1,32]{1,0:T(1,128)S(1)}, f32[1,32]{1,0:T(1,128)}, u32[]{:S(2)}) copy-start(f32[1,32]{1,0:T(1,128)} %param.13) | copy-start | bytes 388
Sparse Core Ops, SparseCore 0:
  15.7 87.9 all-gather.2
  106.5 97.1 all-gather.4
  351.1 28.4 reduce-scatter.1
where the time goes:
time: 391 us; the launch traced here: 388 us
  matrix products  91.8 us (23%)
  other arithmetic  75.4 us (19%)
  waiting for transfers between devices  71.7 us (18%)
  local copies, waits for them, and re-layouts  60.7 us (16%)
  starting transfers between devices  28.7 us (7%)
  blocking collectives  23.8 us (6%)
  loops' own time  22.3 us (6%)
  between operations  13.4 us (3%)
    mul x16, other arithmetic, advance(): weighted = x_block * tail_weight[:, :, None]  38.7 us
    reduce_scatter x1, waiting for transfers between devices, on_device(): shares = lax.psum_scatter(summed, 'tp', scatter_dimension=1, tiled=True)  28.7 us
    all_gather x1, waiting for transfers between devices, on_device(): all_keys = lax.all_gather(key_rows, 'ctx', axis=0, tiled=True)  26.9 us
    all_to_all x1, blocking collectives, on_device(): lax.all_to_all(jnp.stack(pieces_out, axis=1), 'ctx', split_axis=0, concat...  23.8 us
    another operation x1, loops' own time, ssd_blocks(): lax.scan(advance, initial, (x_blocks, step_blocks, b_blocks, c_blocks))  22.3 us
    dot_general x16, matrix products, advance(): jnp.dot(c_block, b_block.T, preferred_element_type=jnp.float32)  22 us
    dot_general x16, matrix products, advance(): jnp.einsum('shp,sn->hpn', weighted, b_float, precision=highest_precision)  21.3 us
    dot_general x16, matrix products, advance(): jnp.einsum('tn,hpn->thp', c_float, carried, precision=highest_precision)  20.8 us
  transfers between devices with their start and end apart: 6, of which 4 were waited for; matrix products, arithmetic and copies ran while one was open for 55% of the time, Pallas kernels for 0%

commit v1 on v0

--- a/solution.py
+++ b/solution.py
@@ -11,6 +11,15 @@
 GCH = 2048
 GCONV = 2560
 highest_precision = lax.Precision.HIGHEST
+touch_the_digits = lambda xx, net_axis: jnp.concatenate(
+    lax.all_to_all(
+        jnp.stack(jnp.split(xx, lax.axis_size(net_axis), axis=0), axis=0),
+        axis_name=net_axis,
+        split_axis=0,
+        concat_axis=0,
+    ),
+    axis=2,
+)
 
 
 def from_behind(shard, axis, by):
@@ -99,9 +108,7 @@
         4 * SPAN,
     )
     pieces_out = [outputs.reshape(sequence, shard_width).astype(jnp.bfloat16)]
-    scanned = lax.all_to_all(
-        jnp.stack(pieces_out, axis=1), "ctx", split_axis=0, concat_axis=2, tiled=True
-    )
+    scanned = touch_the_digits(jnp.stack(pieces_out, axis=1), "ctx")
     gated = scanned.astype(jnp.float32) * jax.nn.silu(projected[:, :, :GCH].astype(jnp.float32))
     normed = (
         gated * lax.rsqrt(jnp.mean(gated * gated, axis=2, keepdims=True) + 1e-05) * norm_gain[None]

time: 391 us -> 368 us (0.941)
  local copies, waits for them, and re-layouts: 60.7 us -> 41.7 us
    unnamed x27 -> x83, local copies, waits for them, and re-layouts: 14.9 us -> 4.8 us
    all_to_all x1 -> x0, local copies, waits for them, and re-layouts: 7.97 us -> none  [on_device(): lax.all_to_all(jnp.stack(pieces_out, axis=1), 'ctx', split_axis=0, concat...]
    unnamed x4 -> x3, other arithmetic: 11.6 us -> 11.5 us
  transfers between devices with their start and end apart: 6 -> 6, of which waited for: 4 -> 4; matrix products, arithmetic and copies ran while one was open for 55% -> 53% of each run, Pallas kernels for 0% -> 0%
where the time goes in v1:
time: 368 us; the launch traced here: 366 us
  matrix products  91.7 us (25%)
  other arithmetic  75.7 us (21%)
  waiting for transfers between devices  69.3 us (19%)
  local copies, waits for them, and re-layouts  41.7 us (11%)
  starting transfers between devices  28.7 us (8%)
  blocking collectives  23.8 us (6%)
  loops' own time  21.3 us (6%)
  between operations  13.6 us (4%)
    mul x16, other arithmetic, advance(): weighted = x_block * tail_weight[:, :, None]  38.7 us
    reduce_scatter x1, waiting for transfers between devices, on_device(): shares = lax.psum_scatter(summed, 'tp', scatter_dimension=1, tiled=True)  28.6 us
    all_gather x1, waiting for transfers between devices, on_device(): all_keys = lax.all_gather(key_rows, 'ctx', axis=0, tiled=True)  24.7 us
    all_to_all x1, blocking collectives, lax.all_to_all(jnp.stack(jnp.split(xx, lax.axis_size(net_axis), axis=0),...  23.8 us
    dot_general x16, matrix products, advance(): jnp.dot(c_block, b_block.T, preferred_element_type=jnp.float32)  22 us
    another operation x1, loops' own time, ssd_blocks(): lax.scan(advance, initial, (x_blocks, step_blocks, b_blocks, c_blocks))  21.3 us
    dot_general x16, matrix products, advance(): jnp.einsum('shp,sn->hpn', weighted, b_float, precision=highest_precision)  21.2 us
    dot_general x16, matrix products, advance(): jnp.einsum('tn,hpn->thp', c_float, carried, precision=highest_precision)  20.7 us
  transfers between devices with their start and end apart: 6, of which 4 were waited for; matrix products, arithmetic and copies ran while one was open for 53% of the time, Pallas kernels for 0%

profile of v1, /device:TPU:1, one launch (start us, length us, event | category | flops | bytes accessed | tf_op | source)
XLA Modules:
  0.0 365.8 jit_solution(17066085548915860691)
XLA Ops:
  6.5 1.4 slice.126
  8.2 4.7 %collective-permute-start = (bf16[3,1,2560]{2,0,1:T(4,128)(2,1)S(1)}, bf16[3,1,2560]{2,0,1:T(4,128)(2,1)S(1)}, u32[]{:S(2)}, u32[]{:S(2)}) collective-permute-start(bf16[3,1,2560]{2,0,1:T(4,128)(2,1)S(1)} %copy.121), channel_id=1, source_target_pairs={{0,4},{4,8},{8,12},{12,16},{16,20},{20,24},{24,28},{28,32},{32,36}... | collective-permute-start | bytes 46088 | tf_op jit(solution)/shard_map/ppermute | solution.py:28
  16.9 13.5 %all-to-all-start = ((bf16[128,1,64]{0,1,2:T(2,128)(2,1)}), bf16[128,1,64]{0,1,2:T(2,128)(2,1)S(1)}, u32[]{:S(2)}, u32[]{:S(2)}) async-start(bf16[128,1,64]{0,1,2:T(2,128)(2,1)} %copy.113), calls=%async_computation | async-start | bytes 65536 | tf_op jit(solution)/shard_map/all_to_all | solution.py:94
  31.7 11.5 %reduce.12 = bf16[2048,128]{1,0:T(8,128)(2,1)S(1)} reduce(bf16[2048,1,128]{2,1,0:T(2,128)(2,1)S(1)} %bitcast.414, bf16[]{:T(256)} %broadcast.159), dimensions={1}, to_apply=%bitcast.348.reduce_sub_computation | reduce | bytes 1048578
  44.2 10.3 %all-to-all-start.1 = ((bf16[64,2,2048]{2,1,0:T(2,128)(2,1)}), bf16[64,2,2048]{2,1,0:T(2,128)(2,1)S(1)}, u32[]{:S(2)}, u32[]{:S(2)}) async-start(bf16[64,2,2048]{2,1,0:T(2,128)(2,1)} %reshape.562), calls=%async_computation.1 | async-start | bytes 1048576 | tf_op jit(solution)/shard_map/all_to_all | solution.py:93
  57.5 14.8 %all-to-all-done.1 = bf16[64,2,2048]{2,1,0:T(2,128)(2,1)S(1)} async-done(((bf16[64,2,2048]{2,1,0:T(2,128)(2,1)}), bf16[64,2,2048]{2,1,0:T(2,128)(2,1)S(1)}, u32[]{:S(2)}, u32[]{:S(2)}) %all-to-all-start.1) | async-done | bytes 524320 | tf_op jit(solution)/shard_map/all_to_all | solution.py:93
  72.3 1.8 reshape.563
  74.2 2.2 bitcast_convert_fusion
  76.3 2.7 copy.117
  79.0 24.7 %all-gather.3.cloned.1.call-done = bf16[8192,1,512]{2,0,1:T(8,128)(2,1)} async-done(((bf16[128,1,512]{2,0,1:T(8,128)(2,1)}), bf16[8192,1,512]{2,0,1:T(8,128)(2,1)}) %all-gather.3.cloned.1.call-update) | async-done | bytes 8388624 | tf_op jit(solution)/shard_map/all_gather | solution.py:96
  103.7 5.9 %fusion.41 = (bf16[8192,1,256]{2,0,1:T(8,128)(2,1)}, bf16[8192,1,256]{2,0,1:T(8,128)(2,1)}) fusion(bf16[8192,1,512]{2,0,1:T(8,128)(2,1)} %all-gather.3.cloned.1.call-done), kind=kLoop, calls=%fused_computation.202 | loop fusion | bytes 16777216 | tf_op jit(solution)/shard_map/slice | solution.py:107
  109.6 184.2 %while.14 = (s32[]{:T(128)}, f32[1,32,256]{2,1,0:T(8,128)S(1)}, bf16[16,512,1,32]{1,3,2,0:T(8,128)(2,1)S(1)}, f32[16,512,1]{1,0,2:T(8,128)S(1)}, f32[1]{0:T(128)...) while((s32[]{:T(128)}, f32[1,32,256]{2,1,0:T(8,128)S(1)}, ...), condition=%wide.region_3.4_spmd.clone.clone, body=%wide.region_0.0_spmd.clone.clone.sunk | while | flops 337266176 | bytes 4002620 | solution.py:66
  113.4 2.4 broadcast_multiply_fusion.2
  115.8 1.4 fusion.69
  124.9 2.4 broadcast_multiply_fusion.2
  127.4 1.4 fusion.69
  136.4 2.4 broadcast_multiply_fusion.2
  138.9 1.4 fusion.69
  147.9 2.4 broadcast_multiply_fusion.2
  150.4 1.4 fusion.69
  159.5 2.4 broadcast_multiply_fusion.2
  161.9 1.4 fusion.69
  171.1 2.4 broadcast_multiply_fusion.2
  173.5 1.4 fusion.69
  182.6 2.4 broadcast_multiply_fusion.2
  185.1 1.4 fusion.69
  194.1 2.4 broadcast_multiply_fusion.2
  196.6 1.4 fusion.69
  205.6 2.4 broadcast_multiply_fusion.2
  208.1 1.4 fusion.69
  217.1 2.4 broadcast_multiply_fusion.2
  219.6 1.4 fusion.69
  228.6 2.4 broadcast_multiply_fusion.2
  231.1 1.4 fusion.69
  240.1 2.4 broadcast_multiply_fusion.2
  242.6 1.4 fusion.69
  251.6 2.4 broadcast_multiply_fusion.2
  254.1 1.4 fusion.69
  263.1 2.4 broadcast_multiply_fusion.2
  265.6 1.4 fusion.69
  274.6 2.4 broadcast_multiply_fusion.2
  277.1 1.4 fusion.69
  286.1 2.4 broadcast_multiply_fusion.2
  288.6 1.4 fusion.69
  294.8 23.8 %all_to_all.23 = bf16[64,128,1,32]{1,3,2,0:T(8,128)(2,1)S(1)} all-to-all(bf16[64,128,1,32]{1,3,2,0:T(8,128)(2,1)S(1)} %constant_dynamic-update-slice_fusion), channel_id=1, replica_groups=mesh['ctx'=64,'tp'=4] {'ctx'}, dimensions={0} | all-to-all | bytes 1048576 | tf_op jit(solution)/shard_map/all_to_all | solution.py:15
  319.3 9.6 %fusion.25 = f32[128,4096]{1,0:T(8,128)} fusion(bf16[1,2048,4096]{2,1,0:T(8,128)(2,1)} %all-gather.5.cloned.1.call-done, f32[2048]{0:T(1024)S(1)} %bitcast.486, f32[128]{0:T(128)S(1)} %add_rsqrt_fusion, f32[128,1,2048]{0,2,1:T(8,128)S(1)} %bitcast.409, bf16[128,1,4640]{0,2,1:T(8,128)(2,1)S(1)} %copy-done.1), kind=kOutput, calls=%fused_computation.38 | convolution fusion | flops 2149842944 | bytes 20455936 | tf_op jit(solution)/shard_map/tgr,grd->td/dot_general | solution.py:116
  328.9 28.6 %reduce-scatter.2.cloned.1.call-done = f32[128,1024]{1,0:T(8,128)} async-done(((f32[128,4096]{1,0:T(8,128)}), f32[128,1024]{1,0:T(8,128)}) %reduce-scatter.2.cloned.1.call-update) | async-done | bytes 524304 | tf_op jit(solution)/shard_map/reduce_scatter | solution.py:122
  357.5 1.8 convert_element_type.96
  (324 shorter events, 113.0 us)
Async XLA Ops:
  6.5 49.0 %copy-start = (f32[1,32]{1,0:T(1,128)S(1)}, f32[1,32]{1,0:T(1,128)}, u32[]{:S(2)}) copy-start(f32[1,32]{1,0:T(1,128)} %param.13) | copy-start | bytes 388
  6.5 6.4 %copy-start.3 = (f32[1,4,2560]{2,1,0:T(4,128)S(1)}, f32[1,4,2560]{2,1,0:T(4,128)}, u32[]{:S(2)}) copy-start(f32[1,4,2560]{2,1,0:T(4,128)} %param.11) | copy-start | bytes 122884
  6.5 6.5 %slice-start = ((bf16[128,1,4640]{0,2,1:T(8,128)(2,1)}), bf16[128,1,2560]{0,2,1:T(8,128)(2,1)S(1)}, s32[]{:S(2)}) async-start(bf16[128,1,4640]{0,2,1:T(8,128)(2,1)} %param.10), calls=%async_computation.7 | async-start | bytes 1310720 | tf_op jit(solution)/shard_map/slice | solution.py:73
  6.5 97.2 %all-gather.3.cloned.1.call-start = ((), (), s32[]{:S(2)}) async-start(), calls=%async_computation.4 | async-start | bytes 8519680 | tf_op jit(solution)/shard_map/all_gather | solution.py:96
  8.2 5.1 %copy-start.4 = (f32[1,2560]{1,0:T(1,128)S(1)}, f32[1,2560]{1,0:T(1,128)}, u32[]{:S(2)}) copy-start(f32[1,2560]{1,0:T(1,128)} %param.12) | copy-start | bytes 30724
  8.2 5.6 %collective-permute-start = (bf16[3,1,2560]{2,0,1:T(4,128)(2,1)S(1)}, bf16[3,1,2560]{2,0,1:T(4,128)(2,1)S(1)}, u32[]{:S(2)}, u32[]{:S(2)}) collective-permute-start(bf16[3,1,2560]{2,0,1:T(4,128)(2,1)S(1)} %copy.121), channel_id=1, source_target_pairs={{0,4},{4,8},{8,12},{12,16},{16,20},{20,24},{24,28},{28,32},{32,36}... | collective-permute-start | bytes 46088 | tf_op jit(solution)/shard_map/ppermute | solution.py:28
  14.0 1.6 copy-start.5
  14.0 1.6 copy-start.1
  16.9 27.3 %all-to-all-start = ((bf16[128,1,64]{0,1,2:T(2,128)(2,1)}), bf16[128,1,64]{0,1,2:T(2,128)(2,1)S(1)}, u32[]{:S(2)}, u32[]{:S(2)}) async-start(bf16[128,1,64]{0,1,2:T(2,128)(2,1)} %copy.113), calls=%async_computation | async-start | bytes 65536 | tf_op jit(solution)/shard_map/all_to_all | solution.py:94
  43.2 13.0 %copy-start.6 = (f32[1,32]{1,0:T(1,128)S(1)}, f32[1,32]{1,0:T(1,128)}, u32[]{:S(2)}) copy-start(f32[1,32]{1,0:T(1,128)} %param.14) | copy-start | bytes 388
  44.2 28.1 %all-to-all-start.1 = ((bf16[64,2,2048]{2,1,0:T(2,128)(2,1)}), bf16[64,2,2048]{2,1,0:T(2,128)(2,1)S(1)}, u32[]{:S(2)}, u32[]{:S(2)}) async-start(bf16[64,2,2048]{2,1,0:T(2,128)(2,1)} %reshape.562), calls=%async_computation.1 | async-start | bytes 1048576 | tf_op jit(solution)/shard_map/all_to_all | solution.py:93
  54.5 264.6 %all-gather.5.cloned.1.call-start = ((), (), s32[]{:S(2)}) async-start(), calls=%async_computation.5 | async-start | bytes 17039360 | tf_op jit(solution)/shard_map/all_gather | solution.py:119
  55.3 302.2 %reduce-scatter.2.cloned.1.call-start = ((), (), s32[]{:S(2)}) async-start(), calls=%async_computation.6 | async-start | bytes 2621440 | tf_op jit(solution)/shard_map/reduce_scatter | solution.py:122
  318.6 0.7 copy-start.2
Sparse Core Ops, SparseCore 0:
  15.7 87.9 all-gather.2
  106.5 96.9 all-gather.4
  329.1 28.4 reduce-scatter.1
